TPU v7x, 256 devices: a whole 4x4x8 slice. The times are simulated.
256 devices in a mesh: fsdp: 32 (over z_hi, x, core), dp: 8 (over y, z_lo).
Axes of the slice: x: 4, y: 4, z: 8 (z_hi: 4, z_lo: 2; z = z_hi * 2 + z_lo), core: 2. Of those that a mesh axis runs over, the one named last changes fastest.
Arguments:
- activations: bfloat16 [65536, 4096], P(('fsdp', 'dp')), may hold values from -6 to 6
- cotangents: bfloat16 [2, 65536, 4096], P(None, ('fsdp', 'dp')), may hold values from -6 to 6
- weights: bfloat16 [2, 4096, 4096], P(None, 'fsdp'), may hold values from -4 to 4
- projectors: bfloat16 [2, 4096, 512], P(None, 'fsdp'), may hold values from -0.09375 to 0.09375
- first_moment: float32 [2, 4096, 512], P(None, 'fsdp'), may hold values from -3 to 3
- second_moment: float32 [2, 4096, 512], P(None, 'fsdp'), may hold values from 0.25 to 4
- matrix_settings: int32 [2, 2], replicated, may hold values from 0 to 512, as said below
Outputs:
- new_weights: bfloat16 [2, 4096, 4096], P(None, 'fsdp')
- new_first: float32 [2, 4096, 512], P(None, 'fsdp')
- new_second: float32 [2, 4096, 512], P(None, 'fsdp')
Inputs may be any that keep to these rules, and one draw needn't show every extreme that they name: `matrix_settings`: column 0 is a rank from 128 to 512, some matrix has rank exactly 512; column 1 is 0 (the projector acts on the activations) or 1 (on the cotangents), and both values occur.
All inputs are finite; a program needn't handle non-finite values.
Results may differ from a plain program's by a relative error of at most 0.0045.
Values may be sent and summed in bfloat16 or wider, within the bound.
No kernel may reach another device: no remote copies, remote signals or barrier semaphores. Data moves between devices by JAX's collectives and lax.ppermute only.
A program may use at most 128 MiB of HBM per device.

v0:
```python
import math
import jax
import jax.numpy as jnp
from jax import lax
from jax.sharding import PartitionSpec as P

BETA_ONE = 0.9
BETA_TWO = 0.95
EPSILON = 1e-08


def on_device(
    activations, cotangents, weights, projectors, first_moment, second_moment, matrix_settings
):
    rank_max = projectors.shape[2]
    token_local = activations.shape[0]
    token_total = token_local * lax.axis_size("fsdp") * lax.axis_size("dp")
    grad_scale = 1.0 / math.sqrt(token_total)
    rank_columns = jnp.arange(rank_max)
    weight_list, first_list, second_list = ([], [], [])
    for matrix_index in range(cotangents.shape[0]):
        live_mask = (rank_columns < matrix_settings[matrix_index, 0])[None, :]
        on_inputs = matrix_settings[matrix_index, 1] == 0
        proj_local = jnp.where(live_mask, projectors[matrix_index], jnp.zeros((), jnp.bfloat16))
        grads_out = cotangents[matrix_index]
        projected_side = jnp.where(on_inputs, activations, grads_out)
        other_side = jnp.where(on_inputs, grads_out, activations)
        shard_piece = lax.all_gather(proj_local, "fsdp", axis=0, tiled=True)
        coeff_sum = jnp.dot(projected_side, shard_piece, preferred_element_type=jnp.float32)
        coeff_sum, full_projector = (coeff_sum, shard_piece)
        coeffs = coeff_sum.astype(jnp.bfloat16)
        partial_sums = lax.psum_scatter(
            lax.dot_general(
                other_side, coeffs, (((0,), (0,)), ((), ())), preferred_element_type=jnp.float32
            ),
            "fsdp",
            scatter_dimension=0,
            tiled=True,
        )
        projected = (
            lax.psum(partial_sums.astype(jnp.bfloat16), "dp").astype(jnp.float32) * grad_scale
        )
        moment_one = jnp.where(
            live_mask, BETA_ONE * first_moment[matrix_index] + (1.0 - BETA_ONE) * projected, 0.0
        )
        moment_two = jnp.where(
            live_mask,
            BETA_TWO * second_moment[matrix_index] + (1.0 - BETA_TWO) * projected * projected,
            0.0,
        )
        normalized = jnp.where(
            live_mask, moment_one / (jnp.sqrt(moment_two) + EPSILON), 0.0
        ).astype(jnp.bfloat16)
        update = lax.dot_general(
            normalized, full_projector, (((1,), (1,)), ((), ())), preferred_element_type=jnp.float32
        )
        weight_list.append(
            (weights[matrix_index].astype(jnp.float32) - update).astype(jnp.bfloat16)
        )
        first_list.append(moment_one)
        second_list.append(moment_two)
    return (jnp.stack(weight_list), jnp.stack(first_list), jnp.stack(second_list))


def solution(mesh):
    return jax.shard_map(
        on_device,
        mesh=mesh,
        in_specs=(
            P(("fsdp", "dp"), None),
            P(None, ("fsdp", "dp"), None),
            P(None, "fsdp", None),
            P(None, "fsdp", None),
            P(None, "fsdp", None),
            P(None, "fsdp", None),
            P(),
        ),
        out_specs=(P(None, "fsdp", None), P(None, "fsdp", None), P(None, "fsdp", None)),
        check_vma=False,
    )
```

profile of v0, /device:TPU:2, one launch (start us, length us, event | category | flops | bytes accessed | tf_op | source)
XLA Modules:
  0.0 480.4 jit_solution(6036514137004158276)
XLA Ops:
  7.2 0.0 all-gather.5.cloned.1.call-start
  7.2 1.5 fusion.56
  8.7 1.3 iota_compare_fusion
  10.0 1.7 bitcast_select_fusion.17
  11.7 0.0 all-gather.5.cloned.1.call-update
  11.7 0.0 all-gather.3.cloned.1.call-start
  11.8 0.7 all-gather.3.cloned.1.call-update
  12.5 0.0 reduce-scatter.5.cloned.1.call-start
  13.2 61.6 %all-gather.5.cloned.1.call-done = bf16[4096,512]{1,0:T(8,128)(2,1)} async-done(((bf16[128,512]{1,0:T(8,128)(2,1)}), bf16[4096,512]{1,0:T(8,128)(2,1)}) %all-gather.5.cloned.1.call-update) | async-done | bytes 4194320 | tf_op jit(solution)/shard_map/all_gather | solution.py:28
  74.8 9.8 %fusion.4 = f32[4096,512]{1,0:T(8,128)} fusion(bf16[256,4096]{1,0:T(8,128)(2,1)} %param.7, pred[]{:T(512)} %bitcast.11, bf16[2,256,4096]{2,1,0:T(8,128)(2,1)} %param.8, bf16[4096,512]{1,0:T(8,128)(2,1)} %all-gather.5.cloned.1.call-done), kind=kOutput, calls=%fused_computation.9 | convolution fusion | flops 2149711872 | bytes 20972544 | tf_op jit(solution)/shard_map/dot_general | solution.py:33
  84.6 0.0 reduce-scatter.5.cloned.1.call-update
  84.6 0.0 reduce-scatter.3.cloned.1.call-start
  85.5 50.9 %all-gather.3.cloned.1.call-done = bf16[4096,512]{1,0:T(8,128)(2,1)} async-done(((bf16[128,512]{1,0:T(8,128)(2,1)}), bf16[4096,512]{1,0:T(8,128)(2,1)}) %all-gather.3.cloned.1.call-update) | async-done | bytes 4194320 | tf_op jit(solution)/shard_map/all_gather | solution.py:28
  136.4 9.2 %fusion.6 = f32[4096,512]{1,0:T(8,128)} fusion(bf16[256,4096]{1,0:T(8,128)(2,1)S(1)} %copy-done, pred[]{:T(512)} %bitcast.3, bf16[2,256,4096]{2,1,0:T(8,128)(2,1)} %param.8, bf16[4096,512]{1,0:T(8,128)(2,1)} %all-gather.3.cloned.1.call-done), kind=kOutput, calls=%fused_computation.13 | convolution fusion | flops 2149711872 | bytes 20972544 | tf_op jit(solution)/shard_map/dot_general | solution.py:33
  145.6 0.0 reduce-scatter.3.cloned.1.call-update
  145.6 0.0 all-reduce.3.cloned.1.call-start
  145.7 113.7 %reduce-scatter.5.cloned.1.call-done = f32[128,512]{1,0:T(8,128)} async-done(((f32[4096,512]{1,0:T(8,128)}), f32[128,512]{1,0:T(8,128)}) %reduce-scatter.5.cloned.1.call-update) | async-done | bytes 262160 | tf_op jit(solution)/shard_map/reduce_scatter | solution.py:32
  259.4 1.6 convert_element_type.52
  261.0 121.5 %reduce-scatter.3.cloned.1.call-done = f32[128,512]{1,0:T(8,128)} async-done(((f32[4096,512]{1,0:T(8,128)}), f32[128,512]{1,0:T(8,128)}) %reduce-scatter.3.cloned.1.call-update) | async-done | bytes 262160 | tf_op jit(solution)/shard_map/reduce_scatter | solution.py:32
  382.5 1.6 convert_element_type.45
  384.1 0.0 all-reduce.3.cloned.1.call-update
  384.2 79.3 %all-reduce.3.cloned.1.call-done = (bf16[128,512]{1,0:T(8,128)(2,1)}, bf16[128,512]{1,0:T(8,128)(2,1)}) async-done(((bf16[128,512]{1,0:T(8,128)(2,1)}, bf16[128,512]{1,0:T(8,128)(2,1)}), (bf16[128,512]{1,0:T(8,128)(2,1)}, bf16[128,512]{1,0:T(8,128)(2,1)})) %all-reduce.3.cloned.1.call-update) | async-done | bytes 262160 | tf_op jit(solution)/shard_map/psum | solution.py:41
  463.5 0.0 copy-done.3
  463.5 1.2 fusion.36
  464.7 0.0 copy-done.5
  464.8 0.0 copy-start.6
  464.8 4.1 fusion.3
  468.9 0.3 copy-done.6
  469.2 1.5 fusion.2
  470.7 1.5 pad_maximum_fusion
  472.2 0.8 pad_maximum_fusion.1
  473.0 0.8 pad_maximum_fusion.2
  (10 shorter events, 0.0 us)
Async XLA Ops:
  7.2 67.7 %all-gather.5.cloned.1.call-start = ((), (), s32[]{:S(2)}) async-start(), calls=%async_computation.4 | async-start | bytes 4325376 | tf_op jit(solution)/shard_map/all_gather | solution.py:28
  11.7 124.7 %all-gather.3.cloned.1.call-start = ((), (), s32[]{:S(2)}) async-start(), calls=%async_computation.2 | async-start | bytes 4325376 | tf_op jit(solution)/shard_map/all_gather | solution.py:28
  12.5 246.9 %reduce-scatter.5.cloned.1.call-start = ((), (), s32[]{:S(2)}) async-start(), calls=%async_computation.5 | async-start | bytes 8650752 | tf_op jit(solution)/shard_map/reduce_scatter | solution.py:32
  84.6 51.8 %copy-start = (bf16[256,4096]{1,0:T(8,128)(2,1)S(1)}, bf16[256,4096]{1,0:T(8,128)(2,1)}, u32[]{:S(2)}) copy-start(bf16[256,4096]{1,0:T(8,128)(2,1)} %param.7) | copy-start | bytes 6291460
  84.6 297.9 %reduce-scatter.3.cloned.1.call-start = ((), (), s32[]{:S(2)}) async-start(), calls=%async_computation.3 | async-start | bytes 8650752 | tf_op jit(solution)/shard_map/reduce_scatter | solution.py:32
  145.6 317.9 %copy-start.2 = (f32[2,128,512]{2,1,0:T(8,128)S(1)}, f32[2,128,512]{2,1,0:T(8,128)}, u32[]{:S(2)}) copy-start(f32[2,128,512]{2,1,0:T(8,128)} %param.11) | copy-start | bytes 1572868
  145.6 317.9 %copy-start.3 = (f32[2,128,512]{2,1,0:T(8,128)S(1)}, f32[2,128,512]{2,1,0:T(8,128)}, u32[]{:S(2)}) copy-start(f32[2,128,512]{2,1,0:T(8,128)} %param.12) | copy-start | bytes 1572868
  145.6 317.9 %all-reduce.3.cloned.1.call-start = ((), (), s32[]{:S(2)}) async-start(), calls=%async_computation.6 | async-start | bytes 524288 | tf_op jit(solution)/shard_map/psum | solution.py:41
  463.5 1.2 copy-start.5
  464.7 4.2 copy-start.1
  464.7 4.2 copy-start.4
  464.8 4.5 copy-start.6
Sparse Core Ops, SparseCore 0:
  11.8 62.9 all-gather.4
  78.0 58.3 all-gather.2
  140.4 118.9 reduce-scatter.4
  263.3 119.2 reduce-scatter.2
  385.6 77.8 all-reduce.2
where the time goes:
time: 481 us; the launch traced here: 480 us
  waiting for transfers between devices  428 us (89%)
  matrix products  24.5 us (5%)
  between operations  15.3 us (3%)
  other arithmetic  10.6 us (2%)
    reduce_scatter x2, waiting for transfers between devices, on_device(): lax.psum_scatter(lax.dot_general(other_side, coeffs, (((0,), (0,)), ((),...  235 us
    all_gather x2, waiting for transfers between devices, on_device(): shard_piece = lax.all_gather(proj_local, 'fsdp', axis=0, tiled=True)  113 us
    psum x1, waiting for transfers between devices, on_device(): lax.psum(partial_sums.astype(jnp.bfloat16), 'dp').astype(jnp.float32)  79.3 us
    dot_general x2, matrix products, on_device(): lax.dot_general(other_side, coeffs, (((0,), (0,)), ((), ())), preferred_e...  18.9 us
  transfers between devices with their start and end apart: 5, of which 5 were waited for; matrix products, arithmetic and copies ran while one was open for 4% of the time, Pallas kernels for 0%

commit v1 on v0

--- a/solution.py
+++ b/solution.py
@@ -25,7 +25,9 @@
         grads_out = cotangents[matrix_index]
         projected_side = jnp.where(on_inputs, activations, grads_out)
         other_side = jnp.where(on_inputs, grads_out, activations)
-        shard_piece = lax.all_gather(proj_local, "fsdp", axis=0, tiled=True)
+        shard_piece = jnp.concatenate(
+            lax.all_to_all(jnp.stack([proj_local] * lax.axis_size("fsdp")), "fsdp", 0, 0), axis=0
+        )
         coeff_sum = jnp.dot(projected_side, shard_piece, preferred_element_type=jnp.float32)
         coeff_sum, full_projector = (coeff_sum, shard_piece)
         coeffs = coeff_sum.astype(jnp.bfloat16)

time: 481 us -> 517 us (1.075)
  starting transfers between devices: 0.2 us -> 17.4 us
  waiting for transfers between devices: 428 us -> 442 us
    all_to_all x0 -> x2, waiting for transfers between devices: none -> 223 us  [on_device(): lax.all_to_all(jnp.stack([proj_local] * lax.axis_size('fsdp')), 'fsdp', 0...]
    all_gather x2 -> x0, waiting for transfers between devices: 113 us -> none  [on_device(): shard_piece = lax.all_gather(proj_local, 'fsdp', axis=0, tiled=True)]
    reduce_scatter x2, waiting for transfers between devices: 235 us -> 139 us  [on_device(): lax.psum_scatter(lax.dot_general(other_side, coeffs, (((0,), (0,)), ((),...]
    all_to_all x0 -> x2, starting transfers between devices: none -> 17.3 us  [on_device(): lax.all_to_all(jnp.stack([proj_local] * lax.axis_size('fsdp')), 'fsdp', 0...]
  transfers between devices with their start and end apart: 5 -> 5, of which waited for: 5 -> 5; matrix products, arithmetic and copies ran while one was open for 4% -> 3% of each run, Pallas kernels for 0% -> 0%
where the time goes in v1:
time: 517 us; the launch traced here: 516 us
  waiting for transfers between devices  442 us (85%)
  matrix products  26.3 us (5%)
  starting transfers between devices  17.4 us (3%)
  between operations  15.1 us (3%)
  other arithmetic  8.88 us (2%)
  local copies, waits for them, and re-layouts  6.33 us (1%)
    all_to_all x2, waiting for transfers between devices, on_device(): lax.all_to_all(jnp.stack([proj_local] * lax.axis_size('fsdp')), 'fsdp', 0...  223 us
    reduce_scatter x2, waiting for transfers between devices, on_device(): lax.psum_scatter(lax.dot_general(other_side, coeffs, (((0,), (0,)), ((),...  139 us
    psum x1, waiting for transfers between devices, on_device(): lax.psum(partial_sums.astype(jnp.bfloat16), 'dp').astype(jnp.float32)  79.6 us
    dot_general x2, matrix products, on_device(): lax.dot_general(other_side, coeffs, (((0,), (0,)), ((), ())), preferred_e...  18.4 us
    all_to_all x2, starting transfers between devices, on_device(): lax.all_to_all(jnp.stack([proj_local] * lax.axis_size('fsdp')), 'fsdp', 0...  17.3 us
  transfers between devices with their start and end apart: 5, of which 5 were waited for; matrix products, arithmetic and copies ran while one was open for 3% of the time, Pallas kernels for 0%

profile of v1, /device:TPU:2, one launch (start us, length us, event | category | flops | bytes accessed | tf_op | source)
XLA Modules:
  0.0 516.2 jit_solution(11248932307391856240)
XLA Ops:
  7.2 1.4 fusion.56
  8.6 1.3 iota_compare_fusion
  9.9 1.0 select_bitcast_fusion.1
  10.9 2.4 stack.30
  13.3 11.8 %all-to-all-start.1 = ((bf16[32,128,512]{2,1,0:T(8,128)(2,1)}), bf16[32,128,512]{2,1,0:T(8,128)(2,1)}, u32[]{:S(2)}, u32[]{:S(2)}) async-start(bf16[32,128,512]{2,1,0:T(8,128)(2,1)} %stack.30), calls=%async_computation.2 | async-start | bytes 8388608 | tf_op jit(solution)/shard_map/all_to_all | solution.py:29
  25.1 0.0 reduce-scatter.5.cloned.1.call-start
  25.8 95.3 %all-to-all-done.1 = bf16[32,128,512]{2,1,0:T(8,128)(2,1)} async-done(((bf16[32,128,512]{2,1,0:T(8,128)(2,1)}), bf16[32,128,512]{2,1,0:T(8,128)(2,1)}, u32[]{:S(2)}, u32[]{:S(2)}) %all-to-all-start.1) | async-done | bytes 4194336 | tf_op jit(solution)/shard_map/all_to_all | solution.py:29
  121.1 0.0 copy-done
  121.1 9.2 %fusion.4 = f32[4096,512]{1,0:T(8,128)} fusion(bf16[256,4096]{1,0:T(8,128)(2,1)S(1)} %copy-done, pred[]{:T(512)} %bitcast.12, bf16[2,256,4096]{2,1,0:T(8,128)(2,1)} %param.8, bf16[4096,512]{1,0:T(8,128)(2,1)} %bitcast.15), kind=kOutput, calls=%fused_computation.9 | convolution fusion | flops 2149711872 | bytes 20972544 | tf_op jit(solution)/shard_map/dot_general | solution.py:35
  130.3 0.0 reduce-scatter.5.cloned.1.call-update
  130.3 2.4 stack.27
  132.7 5.5 %all-to-all-start = ((bf16[32,128,512]{2,1,0:T(8,128)(2,1)}), bf16[32,128,512]{2,1,0:T(8,128)(2,1)}, u32[]{:S(2)}, u32[]{:S(2)}) async-start(bf16[32,128,512]{2,1,0:T(8,128)(2,1)} %stack.27), calls=%async_computation | async-start | bytes 8388608 | tf_op jit(solution)/shard_map/all_to_all | solution.py:29
  138.2 0.0 reduce-scatter.3.cloned.1.call-start
  138.9 128.1 %all-to-all-done = bf16[32,128,512]{2,1,0:T(8,128)(2,1)} async-done(((bf16[32,128,512]{2,1,0:T(8,128)(2,1)}), bf16[32,128,512]{2,1,0:T(8,128)(2,1)}, u32[]{:S(2)}, u32[]{:S(2)}) %all-to-all-start) | async-done | bytes 4194336 | tf_op jit(solution)/shard_map/all_to_all | solution.py:29
  267.0 9.2 %fusion.6 = f32[4096,512]{1,0:T(8,128)} fusion(bf16[256,4096]{1,0:T(8,128)(2,1)S(1)} %copy-done, pred[]{:T(512)} %bitcast.3, bf16[2,256,4096]{2,1,0:T(8,128)(2,1)} %param.8, bf16[4096,512]{1,0:T(8,128)(2,1)} %bitcast.6), kind=kOutput, calls=%fused_computation.13 | convolution fusion | flops 2149711872 | bytes 20972544 | tf_op jit(solution)/shard_map/dot_general | solution.py:35
  276.3 0.0 reduce-scatter.3.cloned.1.call-update
  276.3 0.0 all-reduce.3.cloned.1.call-start
  276.4 17.3 %reduce-scatter.5.cloned.1.call-done = f32[128,512]{1,0:T(8,128)} async-done(((f32[4096,512]{1,0:T(8,128)}), f32[128,512]{1,0:T(8,128)}) %reduce-scatter.5.cloned.1.call-update) | async-done | bytes 262160 | tf_op jit(solution)/shard_map/reduce_scatter | solution.py:34
  293.7 1.6 convert_element_type.52
  295.3 121.8 %reduce-scatter.3.cloned.1.call-done = f32[128,512]{1,0:T(8,128)} async-done(((f32[4096,512]{1,0:T(8,128)}), f32[128,512]{1,0:T(8,128)}) %reduce-scatter.3.cloned.1.call-update) | async-done | bytes 262160 | tf_op jit(solution)/shard_map/reduce_scatter | solution.py:34
  417.2 1.6 convert_element_type.45
  418.8 0.0 all-reduce.3.cloned.1.call-update
  418.8 79.6 %all-reduce.3.cloned.1.call-done = (bf16[128,512]{1,0:T(8,128)(2,1)}, bf16[128,512]{1,0:T(8,128)(2,1)}) async-done(((bf16[128,512]{1,0:T(8,128)(2,1)}, bf16[128,512]{1,0:T(8,128)(2,1)}), (bf16[128,512]{1,0:T(8,128)(2,1)}, bf16[128,512]{1,0:T(8,128)(2,1)})) %all-reduce.3.cloned.1.call-update) | async-done | bytes 262160 | tf_op jit(solution)/shard_map/psum | solution.py:43
  498.4 4.2 fusion.3
  502.5 0.0 copy-done.3
  502.5 0.0 copy-done.5
  502.6 0.0 copy-start.4
  502.6 3.7 fusion.2
  506.3 0.2 fusion.36
  506.5 1.5 pad_maximum_fusion
  508.0 0.8 pad_maximum_fusion.1
  508.8 0.8 pad_maximum_fusion.2
  (8 shorter events, 0.0 us)
Async XLA Ops:
  13.3 107.8 %copy-start = (bf16[256,4096]{1,0:T(8,128)(2,1)S(1)}, bf16[256,4096]{1,0:T(8,128)(2,1)}, u32[]{:S(2)}) copy-start(bf16[256,4096]{1,0:T(8,128)(2,1)} %param.7) | copy-start | bytes 6291460
  13.3 107.8 %all-to-all-start.1 = ((bf16[32,128,512]{2,1,0:T(8,128)(2,1)}), bf16[32,128,512]{2,1,0:T(8,128)(2,1)}, u32[]{:S(2)}, u32[]{:S(2)}) async-start(bf16[32,128,512]{2,1,0:T(8,128)(2,1)} %stack.30), calls=%async_computation.2 | async-start | bytes 8388608 | tf_op jit(solution)/shard_map/all_to_all | solution.py:29
  25.1 268.6 %reduce-scatter.5.cloned.1.call-start = ((), (), s32[]{:S(2)}) async-start(), calls=%async_computation.5 | async-start | bytes 8650752 | tf_op jit(solution)/shard_map/reduce_scatter | solution.py:34
  132.7 134.3 %all-to-all-start = ((bf16[32,128,512]{2,1,0:T(8,128)(2,1)}), bf16[32,128,512]{2,1,0:T(8,128)(2,1)}, u32[]{:S(2)}, u32[]{:S(2)}) async-start(bf16[32,128,512]{2,1,0:T(8,128)(2,1)} %stack.27), calls=%async_computation | async-start | bytes 8388608 | tf_op jit(solution)/shard_map/all_to_all | solution.py:29
  138.2 278.9 %reduce-scatter.3.cloned.1.call-start = ((), (), s32[]{:S(2)}) async-start(), calls=%async_computation.4 | async-start | bytes 8650752 | tf_op jit(solution)/shard_map/reduce_scatter | solution.py:34
  276.3 222.1 %copy-start.1 = (f32[2,128,512]{2,1,0:T(8,128)S(1)}, f32[2,128,512]{2,1,0:T(8,128)}, u32[]{:S(2)}) copy-start(f32[2,128,512]{2,1,0:T(8,128)} %param.11) | copy-start | bytes 1572868
  276.3 222.1 %copy-start.2 = (f32[2,128,512]{2,1,0:T(8,128)S(1)}, f32[2,128,512]{2,1,0:T(8,128)}, u32[]{:S(2)}) copy-start(f32[2,128,512]{2,1,0:T(8,128)} %param.12) | copy-start | bytes 1572868
  276.3 222.1 %all-reduce.3.cloned.1.call-start = ((), (), s32[]{:S(2)}) async-start(), calls=%async_computation.6 | async-start | bytes 524288 | tf_op jit(solution)/shard_map/psum | solution.py:43
  498.4 4.2 copy-start.3
  498.4 4.2 copy-start.5
  502.6 3.7 copy-start.4
Sparse Core Ops, SparseCore 0:
  130.4 163.2 reduce-scatter.4
  297.7 119.3 reduce-scatter.2
  420.4 77.9 all-reduce.2
